TPU v7x, 256 devices: a whole 4x4x8 slice. The times are simulated.
256 devices in a mesh: seq: 32 (over y, x, core), fsdp: 8 (over z).
Axes of the slice: x: 4, y: 4, z: 8, core: 2. Of those that a mesh axis runs over, the one named last changes fastest.
Arguments:
- normed_block_input: bfloat16 [8, 4096, 8192], P('fsdp', 'seq'), may hold values from -6 to 6
- stored_rotated_queries: bfloat16 [8, 4096, 4096], P('fsdp', 'seq'), may hold values from -640 to 640
- stored_rotated_keys: bfloat16 [8, 4096, 512], P('fsdp', 'seq'), may hold values from -4 to 4
- attention_output_gradient: bfloat16 [8, 4096, 4096], P('fsdp', 'seq'), may hold values from -6 to 6
- frozen_value_weight: bfloat16 [8192, 512], P('fsdp'), may hold values from -0.0625 to 0.0625
- adapter_down_weight: bfloat16 [16, 8192], replicated, may hold values from -0.0625 to 0.0625
- adapter_up_weight: bfloat16 [16, 512], replicated, may hold values from -1.5 to 1.5
- packed_document_lengths: int32 [8, 8], P('fsdp'), may hold values from 1 to 1024, 4096 in all within a row
Outputs:
- input_gradient: bfloat16 [8, 4096, 8192], P('fsdp', 'seq')
- rotated_query_gradient: bfloat16 [8, 4096, 4096], P('fsdp', 'seq')
- rotated_key_gradient: bfloat16 [8, 4096, 512], P('fsdp', 'seq')
- adapter_down_gradient: float32 [16, 8192], replicated
- adapter_up_gradient: float32 [16, 512], replicated
Inputs may be any that keep to these rules, and one draw needn't show every extreme that they name: `packed_document_lengths`: row g holds, in order, the lengths of the 8 documents packed into sequence g; they sum to 4096, and in every row the longest has exactly 1024 tokens.
All inputs are finite; a program needn't handle non-finite values.
Results may differ from a plain program's by a relative error of at most 0.0065.
Values may be sent and summed in bfloat16 or wider, within the bound.
A program may use at most 128 MiB of HBM per device.

v0:
```python
import jax
import jax.numpy as jnp
from jax import lax
from jax.sharding import PartitionSpec as P

HEAD_FEATURES = 128
QUERY_HEADS = 32
KEY_VALUE_HEADS = 4
ADAPTER_SCALE = 2.0
NEG_FILL = -1e30


def contract_trailing(left_rows, right_rows):
    return lax.dot_general(
        left_rows, right_rows, (((1,), (1,)), ((), ())), preferred_element_type=jnp.float32
    )


def body(
    normed_block_input,
    stored_rotated_queries,
    stored_rotated_keys,
    attention_output_gradient,
    frozen_value_weight,
    adapter_down_weight,
    adapter_up_weight,
    packed_document_lengths,
):
    token_rows = normed_block_input.shape[1]
    model_features = normed_block_input.shape[2]
    hidden_activations = normed_block_input.reshape(token_rows, model_features)
    seq_count = lax.axis_size("seq")
    fsdp_count = lax.axis_size("fsdp")
    queries_per_group = QUERY_HEADS // KEY_VALUE_HEADS
    key_value_features = KEY_VALUE_HEADS * HEAD_FEATURES
    inverse = HEAD_FEATURES ** (-0.5)
    adapter_projection = contract_trailing(hidden_activations, adapter_down_weight)
    up_widened = adapter_up_weight.astype(jnp.float32)
    adapter_maps = ADAPTER_SCALE * jnp.dot(
        adapter_projection, up_widened, precision=lax.Precision.HIGHEST
    )
    base_value = jnp.dot(
        hidden_activations,
        lax.all_gather(frozen_value_weight, "fsdp", axis=0, tiled=True),
        preferred_element_type=jnp.float32,
    )
    adapter_values = (base_value + adapter_maps).astype(jnp.bfloat16)
    shaped = (token_rows, QUERY_HEADS, HEAD_FEATURES)
    key_broadcast = jnp.repeat(
        stored_rotated_keys.reshape(token_rows, KEY_VALUE_HEADS, HEAD_FEATURES),
        queries_per_group,
        axis=1,
    )
    value_broadcast = jnp.repeat(
        adapter_values.reshape(token_rows, KEY_VALUE_HEADS, HEAD_FEATURES),
        queries_per_group,
        axis=1,
    )
    head_query, head_key, head_value, head_grad = (
        lax.all_to_all(
            stored_rotated_queries.reshape(shaped), "seq", split_axis=1, concat_axis=0, tiled=True
        ),
        lax.all_to_all(key_broadcast, "seq", split_axis=1, concat_axis=0, tiled=True),
        lax.all_to_all(value_broadcast, "seq", split_axis=1, concat_axis=0, tiled=True),
        lax.all_to_all(
            attention_output_gradient.reshape(shaped),
            "seq",
            split_axis=1,
            concat_axis=0,
            tiled=True,
        ),
    )
    seq_len = head_query.shape[0]
    local_heads = head_query.shape[1]
    block_rows = min(512, seq_len)
    key_reach = block_rows + seq_len // 4
    bounds = jnp.cumsum(packed_document_lengths[0])
    places = jnp.arange(seq_len, dtype=jnp.int32)
    segments = jnp.sum((places[:, None] >= bounds[None, :]).astype(jnp.int32), axis=1)
    grad_keys = jnp.zeros((seq_len, local_heads, HEAD_FEATURES), jnp.float32)
    grad_values = jnp.zeros((seq_len, local_heads, HEAD_FEATURES), jnp.float32)
    query_parts = []
    for block_index in range(seq_len // block_rows):
        first_row = block_index * block_rows
        finish = first_row + block_rows
        opening = max(0, finish - key_reach)
        query_block = head_query[first_row:finish]
        grad_block = head_grad[first_row:finish]
        key_block = head_key[opening:finish]
        value_block = head_value[opening:finish]
        scores = (
            jnp.einsum("qhd,khd->hqk", query_block, key_block, preferred_element_type=jnp.float32)
            * inverse
        )
        allowed = (places[opening:finish][None, :] <= places[first_row:finish][:, None]) & (
            segments[opening:finish][None, :] == segments[first_row:finish][:, None]
        )
        scores = jnp.where(allowed[None], scores, NEG_FILL)
        row_peak = jnp.max(scores, axis=2, keepdims=True)
        weights = jnp.exp(scores - row_peak)
        probs_full = weights / jnp.sum(weights, axis=2, keepdims=True)
        probs_low = probs_full.astype(jnp.bfloat16)
        grad_probs = jnp.einsum(
            "qhd,khd->hqk", grad_block, value_block, preferred_element_type=jnp.float32
        )
        row_delta = jnp.sum(probs_full * grad_probs, axis=2, keepdims=True)
        grad_scores = (probs_full * (grad_probs - row_delta)).astype(jnp.bfloat16)
        query_parts.append(
            jnp.einsum("hqk,khd->qhd", grad_scores, key_block, preferred_element_type=jnp.float32)
            * inverse
        )
        key_part = (
            jnp.einsum("hqk,qhd->khd", grad_scores, query_block, preferred_element_type=jnp.float32)
            * inverse
        )
        value_part = jnp.einsum(
            "hqk,qhd->khd", probs_low, grad_block, preferred_element_type=jnp.float32
        )
        grad_keys = lax.dynamic_update_slice_in_dim(
            grad_keys, grad_keys[opening:finish] + key_part, opening, 0
        )
        grad_values = lax.dynamic_update_slice_in_dim(
            grad_values, grad_values[opening:finish] + value_part, opening, 0
        )
    grad_queries = jnp.concatenate(query_parts, axis=0).astype(jnp.bfloat16)
    token_query = lax.all_to_all(grad_queries, "seq", split_axis=0, concat_axis=1, tiled=True)
    rotated_query_gradient = token_query.reshape(1, token_rows, QUERY_HEADS * HEAD_FEATURES)
    token_key_matrix, token_value_matrix = (
        lax.all_to_all(grad_keys, "seq", split_axis=0, concat_axis=1, tiled=True),
        lax.all_to_all(grad_values, "seq", split_axis=0, concat_axis=1, tiled=True),
    )
    per_key_value_head = token_key_matrix.shape[1] // KEY_VALUE_HEADS
    rotated_key_gradient = (
        token_key_matrix.reshape(token_rows, KEY_VALUE_HEADS, per_key_value_head, HEAD_FEATURES)
        .sum(axis=2)
        .reshape(1, token_rows, key_value_features)
        .astype(jnp.bfloat16)
    )
    value_gradient_matrix = (
        token_value_matrix.reshape(token_rows, KEY_VALUE_HEADS, per_key_value_head, HEAD_FEATURES)
        .sum(axis=2)
        .reshape(token_rows, key_value_features)
    )
    value_grad_low = value_gradient_matrix.astype(jnp.bfloat16)
    adapter_rank_gradient = ADAPTER_SCALE * lax.dot_general(
        value_gradient_matrix, up_widened, (((1,), (1,)), ((), ())), precision=lax.Precision.HIGHEST
    )
    reduced_rank_gradient = adapter_rank_gradient.astype(jnp.bfloat16)
    frozen_path_gradient = contract_trailing(
        value_grad_low, lax.all_gather(frozen_value_weight, "fsdp", axis=0, tiled=True)
    )
    input_gradient = (
        frozen_path_gradient
        + jnp.dot(reduced_rank_gradient, adapter_down_weight, preferred_element_type=jnp.float32)
    ).astype(jnp.bfloat16)
    overall_token_count = token_rows * seq_count * fsdp_count
    down_shard = (
        lax.dot_general(
            reduced_rank_gradient,
            hidden_activations,
            (((0,), (0,)), ((), ())),
            preferred_element_type=jnp.float32,
        )
        / overall_token_count
    )
    up_shard = (
        ADAPTER_SCALE
        * jnp.dot(adapter_projection.T, value_gradient_matrix, precision=lax.Precision.HIGHEST)
        / overall_token_count
    )
    adapter_down_gradient, adapter_up_gradient = lax.psum((down_shard, up_shard), ("seq", "fsdp"))
    return (
        input_gradient.reshape(1, token_rows, model_features),
        rotated_query_gradient,
        rotated_key_gradient,
        adapter_down_gradient,
        adapter_up_gradient,
    )


def solution(mesh):
    placed = (
        P("fsdp", "seq", None),
        P("fsdp", "seq", None),
        P("fsdp", "seq", None),
        P("fsdp", "seq", None),
        P("fsdp", None),
        P(),
        P(),
        P("fsdp", None),
    )
    return jax.shard_map(
        body,
        mesh=mesh,
        in_specs=placed,
        out_specs=(
            P("fsdp", "seq", None),
            P("fsdp", "seq", None),
            P("fsdp", "seq", None),
            P(),
            P(),
        ),
        check_vma=False,
    )
```

profile of v0, /device:TPU:2, one launch (start us, length us, event | category | flops | bytes accessed | tf_op | source)
XLA Modules:
  0.0 526.1 jit_solution(7725692542050299921)
XLA Ops:
  8.8 2.3 copy.161
  11.0 7.6 %all-to-all-start.2 = ((bf16[128,32,128]{0,2,1:T(8,128)(2,1)}), bf16[128,32,128]{0,2,1:T(8,128)(2,1)S(1)}, u32[]{:S(2)}, u32[]{:S(2)}) async-start(bf16[128,32,128]{0,2,1:T(8,128)(2,1)} %bitcast.418), calls=%async_computation.2 | async-start | bytes 2097152 | tf_op jit(solution)/shard_map/all_to_all | solution.py:65
  20.5 14.2 %all-to-all-done.2 = bf16[128,32,128]{0,2,1:T(8,128)(2,1)S(1)} async-done(((bf16[128,32,128]{0,2,1:T(8,128)(2,1)}), bf16[128,32,128]{0,2,1:T(8,128)(2,1)S(1)}, u32[]{:S(2)}, u32[]{:S(2)}) %all-to-all-start.2) | async-done | bytes 1048608 | tf_op jit(solution)/shard_map/all_to_all | solution.py:65
  34.6 1.3 broadcast_in_dim.19
  36.0 5.2 all-to-all-start.1
  41.7 2.3 copy.158
  49.0 8.3 %all-to-all-done.1 = bf16[128,32,128]{2,0,1:T(8,128)(2,1)S(1)} async-done(((bf16[128,32,128]{2,0,1:T(8,128)(2,1)}), bf16[128,32,128]{2,0,1:T(8,128)(2,1)S(1)}, u32[]{:S(2)}, u32[]{:S(2)}) %all-to-all-start.1) | async-done | bytes 1048608 | tf_op jit(solution)/shard_map/all_to_all | solution.py:63
  57.3 6.2 %all-to-all-start = ((bf16[128,32,128]{0,2,1:T(8,128)(2,1)}), bf16[128,32,128]{0,2,1:T(8,128)(2,1)}, u32[]{:S(2)}, u32[]{:S(2)}) async-start(bf16[128,32,128]{0,2,1:T(8,128)(2,1)} %bitcast.416), calls=%async_computation | async-start | bytes 2097152 | tf_op jit(solution)/shard_map/all_to_all | solution.py:60
  68.9 1.7 copy.162
  70.5 8.6 %all-to-all-done = bf16[128,32,128]{0,2,1:T(8,128)(2,1)} async-done(((bf16[128,32,128]{0,2,1:T(8,128)(2,1)}), bf16[128,32,128]{0,2,1:T(8,128)(2,1)}, u32[]{:S(2)}, u32[]{:S(2)}) %all-to-all-start) | async-done | bytes 1048608 | tf_op jit(solution)/shard_map/all_to_all | solution.py:60
  79.1 2.2 fusion.117
  81.4 1.6 copy.159
  83.0 1.7 copy.164
  84.7 1.7 copy.163
  86.4 1.7 copy.166
  88.0 1.7 copy.165
  89.7 1.7 copy.168
  91.3 1.7 copy.167
  98.4 1.7 copy.176
  100.0 1.7 copy.175
  101.7 1.4 fusion.121
  103.3 1.5 convolution_bitcast_fusion.14
  104.8 1.5 dynamic_update_slice.48
  115.9 1.5 fusion.17
  118.7 1.5 fusion.19
  120.2 1.6 fusion.69
  121.8 3.1 fusion.39
  124.9 3.1 fusion.41
  128.1 3.1 fusion.43
  131.2 3.1 fusion.45
  134.3 4.7 fusion.56
  140.6 5.1 all-to-all-start.4
  145.7 4.1 fusion.47
  149.8 3.1 fusion.49
  152.9 8.8 %all-to-all-done.4 = bf16[128,32,128]{2,0,1:T(8,128)(2,1)S(1)} async-done(((bf16[128,32,128]{2,0,1:T(8,128)(2,1)}), bf16[128,32,128]{2,0,1:T(8,128)(2,1)S(1)}, u32[]{:S(2)}, u32[]{:S(2)}) %all-to-all-start.4) | async-done | bytes 1048608 | tf_op jit(solution)/shard_map/all_to_all | solution.py:64
  161.8 5.8 %all-to-all-start.3 = ((f32[4096,1,128]{2,1,0:T(1,128)}), f32[4096,1,128]{2,1,0:T(1,128)}, u32[]{:S(2)}, u32[]{:S(2)}) async-start(f32[4096,1,128]{2,1,0:T(1,128)} %bitcast.62), calls=%async_computation.3 | async-start | bytes 4194304 | tf_op jit(solution)/shard_map/all_to_all | solution.py:130
  172.7 2.5 multiply_reduce_fusion.5
  175.2 2.5 multiply_reduce_fusion.4
  183.5 1.4 multiply_reduce_fusion
  186.9 2.7 multiply_convert_fusion.5
  190.9 2.7 multiply_convert_fusion.4
  205.3 2.7 reduce.48
  209.1 1.5 fusion.72
  210.6 1.6 dynamic_update_slice.56
  213.5 2.6 fusion.37
  216.1 2.6 fusion.35
  218.8 7.8 %all-to-all-start.5 = ((bf16[32,2,8192]{2,1,0:T(2,128)(2,1)}), bf16[32,2,8192]{2,1,0:T(2,128)(2,1)S(1)}, u32[]{:S(2)}, u32[]{:S(2)}) async-start(bf16[32,2,8192]{2,1,0:T(2,128)(2,1)} %reshape.801), calls=%async_computation.5 | async-start | bytes 2097152 | tf_op jit(solution)/shard_map/all_to_all | solution.py:126
  226.6 3.3 fusion.33
  229.9 2.8 fusion.31
  232.8 2.7 fusion.29
  235.4 2.6 fusion.27
  238.1 4.4 all-to-all-done.5
  242.5 5.9 %all-to-all-start.6 = ((f32[4096,1,128]{2,1,0:T(1,128)}), f32[4096,1,128]{2,1,0:T(1,128)}, u32[]{:S(2)}, u32[]{:S(2)}) async-start(f32[4096,1,128]{2,1,0:T(1,128)} %bitcast.139), calls=%async_computation.6 | async-start | bytes 4194304 | tf_op jit(solution)/shard_map/all_to_all | solution.py:129
  248.5 2.4 reduce_sum.180
  253.7 90.2 %psum.15 = f32[16,512]{1,0:T(8,128)} all-reduce(f32[16,512]{1,0:T(8,128)S(1)} %convolution_multiply_fusion.25), channel_id=1, replica_groups=mesh['seq'=32,'fsdp'=8] {'seq','fsdp'}, use_global_device_ids=true, to_apply=%region_29.30 | all-reduce | flops 8192 | bytes 65536 | tf_op jit(solution)/shard_map/psum | solution.py:171
  344.0 6.3 %fusion.105 = f32[128,8192]{1,0:T(8,128)S(1)} fusion(bf16[8192,512]{1,0:T(8,128)(2,1)} %all-gather.2.cloned.1.call-done, f32[128,512]{0,1:T(8,128)S(1)} %bitcast.414), kind=kOutput, calls=%fused_computation.176 | convolution fusion | flops 1073807360 | bytes 12845056 | tf_op jit(solution)/shard_map/dot_general | solution.py:14
  350.3 2.1 fusion.1
  352.3 3.4 reshape.802
  355.7 1.7 copy.200
  357.5 1.3 copy.188
  358.8 2.3 copy.191
  361.1 1.7 reduce_sum.189
  363.7 152.6 %all-reduce.4.cloned.1.call-done = f32[16,8192]{1,0:T(8,128)} async-done(((f32[16,8192]{1,0:T(8,128)}), f32[16,8192]{1,0:T(8,128)}) %all-reduce.4.cloned.1.call-update) | async-done | bytes 524304 | tf_op jit(solution)/shard_map/psum | solution.py:171
  516.3 1.9 copy.227
  (358 shorter events, 62.4 us)
Async XLA Ops:
  8.0 57.4 %copy-start = (bf16[1,128,8192]{2,1,0:T(8,128)(2,1)S(1)}, bf16[1,128,8192]{2,1,0:T(8,128)(2,1)}, u32[]{:S(2)}) copy-start(bf16[1,128,8192]{2,1,0:T(8,128)(2,1)} %param.8) | copy-start | bytes 6291460
  8.0 10.6 %copy-start.59 = (bf16[1,128,512]{2,1,0:T(8,128)(2,1)S(1)}, bf16[1,128,512]{2,1,0:T(8,128)(2,1)}, u32[]{:S(2)}) copy-start(bf16[1,128,512]{2,1,0:T(8,128)(2,1)} %param.10) | copy-start | bytes 393220
  8.0 126.3 %all-gather.2.cloned.1.call-start = ((), (), s32[]{:S(2)}) async-start(), calls=%async_computation.7 | async-start | bytes 9437184 | tf_op jit(solution)/shard_map/all_gather | solution.py:150
  11.0 23.6 %all-to-all-start.2 = ((bf16[128,32,128]{0,2,1:T(8,128)(2,1)}), bf16[128,32,128]{0,2,1:T(8,128)(2,1)S(1)}, u32[]{:S(2)}, u32[]{:S(2)}) async-start(bf16[128,32,128]{0,2,1:T(8,128)(2,1)} %bitcast.418), calls=%async_computation.2 | async-start | bytes 2097152 | tf_op jit(solution)/shard_map/all_to_all | solution.py:65
  18.7 25.3 %copy-start.135 = (s32[1,8]{1,0:T(1,128)S(1)}, s32[1,8]{1,0:T(1,128)}, u32[]{:S(2)}) copy-start(s32[1,8]{1,0:T(1,128)} %param.15) | copy-start | bytes 100
  36.0 29.4 %copy-start.34 = (bf16[16,8192]{1,0:T(8,128)(2,1)S(1)}, bf16[16,8192]{1,0:T(8,128)(2,1)}, u32[]{:S(2)}) copy-start(bf16[16,8192]{1,0:T(8,128)(2,1)} %param.13) | copy-start | bytes 786436
  36.0 21.3 %all-to-all-start.1 = ((bf16[128,32,128]{2,0,1:T(8,128)(2,1)}), bf16[128,32,128]{2,0,1:T(8,128)(2,1)S(1)}, u32[]{:S(2)}, u32[]{:S(2)}) async-start(bf16[128,32,128]{2,0,1:T(8,128)(2,1)} %bitcast.417), calls=%async_computation.1 | async-start | bytes 2097152 | tf_op jit(solution)/shard_map/all_to_all | solution.py:63
  49.0 19.8 %copy-start.44 = (s32[4096]{0:T(1024)}, s32[4096]{0:T(1024)S(1)}, u32[]{:S(2)}) copy-start(s32[4096]{0:T(1024)S(1)} %convert_reduce_fusion) | copy-start | bytes 49156
  57.3 21.9 %all-to-all-start = ((bf16[128,32,128]{0,2,1:T(8,128)(2,1)}), bf16[128,32,128]{0,2,1:T(8,128)(2,1)}, u32[]{:S(2)}, u32[]{:S(2)}) async-start(bf16[128,32,128]{0,2,1:T(8,128)(2,1)} %bitcast.416), calls=%async_computation | async-start | bytes 2097152 | tf_op jit(solution)/shard_map/all_to_all | solution.py:60
  63.5 4.5 copy-start.30
  68.9 32.8 %copy-start.126 = (s32[512]{0:T(512)S(1)}, s32[512]{0:T(512)}, u32[]{:S(2)}) copy-start(s32[512]{0:T(512)} %get-tuple-element.55) | copy-start | bytes 6148
  68.9 32.8 %copy-start.127 = (s32[512]{0:T(512)S(1)}, s32[512]{0:T(512)}, u32[]{:S(2)}) copy-start(s32[512]{0:T(512)} %get-tuple-element.94) | copy-start | bytes 6148
  103.0 3.2 copy-start.27
  103.1 3.2 copy-start.90
  103.3 3.0 copy-start.92
  103.3 3.0 copy-start.42
  103.3 3.0 slice-start
  103.3 3.0 copy-start.57
  107.0 13.1 %copy-start.14 = (f32[512,1024]{1,0:T(8,128)}, f32[512,1024]{1,0:T(8,128)S(1)}, u32[]{:S(2)}) copy-start(f32[512,1024]{1,0:T(8,128)S(1)} %get-tuple-element.65) | copy-start | bytes 6291460
  108.2 3.4 copy-start.51
  108.2 5.0 copy-start.49
  108.2 6.6 %copy-start.47 = (bf16[12,128,1,128]{3,1,0,2:T(8,128)(2,1)}, bf16[12,128,1,128]{3,1,0,2:T(8,128)(2,1)S(1)}, u32[]{:S(2)}) copy-start(bf16[12,128,1,128]{3,1,0,2:T(8,128)(2,1)S(1)} %get-tuple-element.27) | copy-start | bytes 1179652
  108.2 9.2 %copy-start.45 = (bf16[12,128,1,128]{3,1,0,2:T(8,128)(2,1)}, bf16[12,128,1,128]{3,1,0,2:T(8,128)(2,1)S(1)}, u32[]{:S(2)}) copy-start(bf16[12,128,1,128]{3,1,0,2:T(8,128)(2,1)S(1)} %get-tuple-element.26) | copy-start | bytes 1179652
  109.3 12.5 %copy-start.12 = (f32[512,1536]{1,0:T(8,128)}, f32[512,1536]{1,0:T(8,128)S(1)}, u32[]{:S(2)}) copy-start(f32[512,1536]{1,0:T(8,128)S(1)} %get-tuple-element.67) | copy-start | bytes 9437188
  109.3 12.5 %copy-start.105 = (f32[512]{0:T(512)}, f32[512]{0:T(512)S(1)}, u32[]{:S(2)}) copy-start(f32[512]{0:T(512)S(1)} %get-tuple-element.66) | copy-start | bytes 6148
  109.9 11.9 %copy-start.116 = (f32[512]{0:T(512)}, f32[512]{0:T(512)S(1)}, u32[]{:S(2)}) copy-start(f32[512]{0:T(512)S(1)} %fusion.9) | copy-start | bytes 6148
  110.9 14.0 %copy-start.10 = (f32[512,1536]{1,0:T(8,128)}, f32[512,1536]{1,0:T(8,128)S(1)}, u32[]{:S(2)}) copy-start(f32[512,1536]{1,0:T(8,128)S(1)} %get-tuple-element.69) | copy-start | bytes 9437188
  111.0 14.0 %copy-start.103 = (f32[512]{0:T(512)}, f32[512]{0:T(512)S(1)}, u32[]{:S(2)}) copy-start(f32[512]{0:T(512)S(1)} %get-tuple-element.68) | copy-start | bytes 6148
  111.5 13.4 %copy-start.114 = (f32[512]{0:T(512)}, f32[512]{0:T(512)S(1)}, u32[]{:S(2)}) copy-start(f32[512]{0:T(512)S(1)} %fusion.11) | copy-start | bytes 6148
  112.6 15.5 %copy-start.5 = (f32[512,1536]{1,0:T(8,128)}, f32[512,1536]{1,0:T(8,128)S(1)}, u32[]{:S(2)}) copy-start(f32[512,1536]{1,0:T(8,128)S(1)} %get-tuple-element.71) | copy-start | bytes 9437188
  112.6 15.5 %copy-start.98 = (f32[512]{0:T(512)}, f32[512]{0:T(512)S(1)}, u32[]{:S(2)}) copy-start(f32[512]{0:T(512)S(1)} %get-tuple-element.70) | copy-start | bytes 6148
  113.2 14.9 %copy-start.110 = (f32[512]{0:T(512)}, f32[512]{0:T(512)S(1)}, u32[]{:S(2)}) copy-start(f32[512]{0:T(512)S(1)} %fusion.13) | copy-start | bytes 6148
  114.2 17.0 %copy-start.3 = (f32[512,1536]{1,0:T(8,128)}, f32[512,1536]{1,0:T(8,128)S(1)}, u32[]{:S(2)}) copy-start(f32[512,1536]{1,0:T(8,128)S(1)} %get-tuple-element.73) | copy-start | bytes 9437188
  114.3 16.9 %copy-start.96 = (f32[512]{0:T(512)}, f32[512]{0:T(512)S(1)}, u32[]{:S(2)}) copy-start(f32[512]{0:T(512)S(1)} %get-tuple-element.72) | copy-start | bytes 6148
  114.8 16.4 %copy-start.108 = (f32[512]{0:T(512)}, f32[512]{0:T(512)S(1)}, u32[]{:S(2)}) copy-start(f32[512]{0:T(512)S(1)} %fusion.15) | copy-start | bytes 6148
  118.7 3.1 copy-start.7
  118.7 3.1 copy-start.100
  121.8 3.1 copy-start.69
  124.9 3.1 copy-start.67
  128.1 3.1 copy-start.65
  134.3 4.7 copy-start.75
  134.3 4.7 copy-start.76
  140.6 21.2 %all-to-all-start.4 = ((bf16[128,32,128]{2,0,1:T(8,128)(2,1)}), bf16[128,32,128]{2,0,1:T(8,128)(2,1)S(1)}, u32[]{:S(2)}, u32[]{:S(2)}) async-start(bf16[128,32,128]{2,0,1:T(8,128)(2,1)} %bitcast.419), calls=%async_computation.4 | async-start | bytes 2097152 | tf_op jit(solution)/shard_map/all_to_all | solution.py:64
  145.7 4.2 copy-start.8
  145.7 4.1 copy-start.61
  145.7 4.1 copy-start.101
  145.7 4.1 copy-start.112
  161.8 57.0 %all-to-all-start.3 = ((f32[4096,1,128]{2,1,0:T(1,128)}), f32[4096,1,128]{2,1,0:T(1,128)}, u32[]{:S(2)}, u32[]{:S(2)}) async-start(f32[4096,1,128]{2,1,0:T(1,128)} %bitcast.62), calls=%async_computation.3 | async-start | bytes 4194304 | tf_op jit(solution)/shard_map/all_to_all | solution.py:130
  189.7 4.0 copy-start.16
  209.1 3.1 copy-start.32
  209.1 3.1 copy-start.43
  209.1 4.3 copy-start.17
  209.1 4.3 copy-start.39
  212.2 3.9 copy-start.20
  212.2 3.9 copy-start.41
  218.8 23.7 %all-to-all-start.5 = ((bf16[32,2,8192]{2,1,0:T(2,128)(2,1)}), bf16[32,2,8192]{2,1,0:T(2,128)(2,1)S(1)}, u32[]{:S(2)}, u32[]{:S(2)}) async-start(bf16[32,2,8192]{2,1,0:T(2,128)(2,1)} %reshape.801), calls=%async_computation.5 | async-start | bytes 2097152 | tf_op jit(solution)/shard_map/all_to_all | solution.py:126
  226.6 3.3 copy-start.22
  226.6 6.1 %copy-start.24 = (bf16[512,1536]{1,0:T(8,128)(2,1)S(1)}, bf16[512,1536]{1,0:T(8,128)(2,1)}, u32[]{:S(2)}) copy-start(bf16[512,1536]{1,0:T(8,128)(2,1)} %copy-done.23) | copy-start | bytes 4718596
  229.9 5.5 %copy-start.26 = (bf16[512,1536]{1,0:T(8,128)(2,1)S(1)}, bf16[512,1536]{1,0:T(8,128)(2,1)}, u32[]{:S(2)}) copy-start(bf16[512,1536]{1,0:T(8,128)(2,1)} %copy-done.25) | copy-start | bytes 4718596
  229.9 5.5 %copy-start.37 = (bf16[4,128,1,128]{3,1,0,2:T(8,128)(2,1)S(1)}, bf16[4,128,1,128]{3,1,0,2:T(8,128)(2,1)}, u32[]{:S(2)}) copy-start(bf16[4,128,1,128]{3,1,0,2:T(8,128)(2,1)} %copy.175) | copy-start | bytes 393220
  242.5 9.5 %copy-start.77 = (bf16[16,512]{1,0:T(8,128)(2,1)S(1)}, bf16[16,512]{1,0:T(8,128)(2,1)}, u32[]{:S(2)}) copy-start(bf16[16,512]{1,0:T(8,128)(2,1)} %param.14) | copy-start | bytes 49156
  242.5 118.6 %all-to-all-start.6 = ((f32[4096,1,128]{2,1,0:T(1,128)}), f32[4096,1,128]{2,1,0:T(1,128)}, u32[]{:S(2)}, u32[]{:S(2)}) async-start(f32[4096,1,128]{2,1,0:T(1,128)} %bitcast.139), calls=%async_computation.6 | async-start | bytes 4194304 | tf_op jit(solution)/shard_map/all_to_all | solution.py:129
  248.4 267.9 %all-reduce.4.cloned.1.call-start = ((), (), s32[]{:S(2)}) async-start(), calls=%async_computation.8 | async-start | bytes 1048576 | tf_op jit(solution)/shard_map/psum | solution.py:171
  344.0 6.3 %copy-start.35 = (bf16[16,8192]{1,0:T(8,128)(2,1)S(1)}, bf16[16,8192]{1,0:T(8,128)(2,1)}, u32[]{:S(2)}) copy-start(bf16[16,8192]{1,0:T(8,128)(2,1)} %param.13) | copy-start | bytes 786436
  (82 other events, 153.1 us)
Sparse Core Ops, SparseCore 0:
  10.6 97.0 all-gather.1
Sparse Core Ops, SparseCore 1:
  255.0 261.3 all-reduce.3
where the time goes:
time: 530 us; the launch traced here: 526 us
  waiting for transfers between devices  198 us (37%)
  blocking collectives  90.2 us (17%)
  matrix products  86.9 us (16%)
  local copies, waits for them, and re-layouts  58.5 us (11%)
  starting transfers between devices  43.8 us (8%)
  other arithmetic  31.5 us (6%)
  between operations  17.6 us (3%)
    psum x1, waiting for transfers between devices, body(): lax.psum((down_shard, up_shard), ('seq', 'fsdp'))  153 us
    psum x1, blocking collectives, body(): lax.psum((down_shard, up_shard), ('seq', 'fsdp'))  90.2 us
    dot_general x8, matrix products, body(): jnp.einsum('hqk,qhd->khd', probs_low, grad_block, preferred_element_type=...  22.6 us
    unnamed x280, local copies, waits for them, and re-layouts  22.2 us
    dot_general x8, matrix products, body(): jnp.einsum('hqk,qhd->khd', grad_scores, query_block, preferred_element_ty...  19.5 us
    all_to_all x1, waiting for transfers between devices, body(): lax.all_to_all(attention_output_gradient.reshape(shaped), 'seq', split_ax...  14.2 us
    slice x9, local copies, waits for them, and re-layouts, body(): query_block = head_query[first_row:finish]  13.6 us
    slice x9, local copies, waits for them, and re-layouts, body(): grad_block = head_grad[first_row:finish]  11.4 us
  transfers between devices with their start and end apart: 9, of which 6 were waited for; matrix products, arithmetic and copies ran while one was open for 31% of the time, Pallas kernels for 0%

commit v1 on v0

--- a/solution.py
+++ b/solution.py
@@ -168,7 +168,9 @@
         * jnp.dot(adapter_projection.T, value_gradient_matrix, precision=lax.Precision.HIGHEST)
         / overall_token_count
     )
-    adapter_down_gradient, adapter_up_gradient = lax.psum((down_shard, up_shard), ("seq", "fsdp"))
+    adapter_down_gradient, adapter_up_gradient = lax.psum(
+        lax.psum((down_shard, up_shard), "seq"), "fsdp"
+    )
     return (
         input_gradient.reshape(1, token_rows, model_features),
         rotated_query_gradient,

time: 530 us -> 508 us (0.958)
  waiting for transfers between devices: 198 us -> 97.1 us
  blocking collectives: 90.2 us -> 168 us
    psum x1 -> x2, waiting for transfers between devices: 153 us -> 52.1 us  [the longest x1 52.1 us: body(): lax.psum(lax.psum((down_shard, up_shard), 'seq'), 'fsdp')]
    psum x1 -> x2, blocking collectives: 90.2 us -> 168 us  [the longest x1 134 us: body(): lax.psum((down_shard, up_shard), 'seq')]
  transfers between devices with their start and end apart: 9 -> 10, of which waited for: 6 -> 6; matrix products, arithmetic and copies ran while one was open for 31% -> 32% of each run, Pallas kernels for 0% -> 0%
where the time goes in v1:
time: 508 us; the launch traced here: 503 us
  blocking collectives  168 us (33%)
  waiting for transfers between devices  97.1 us (19%)
  matrix products  86.9 us (17%)
  local copies, waits for them, and re-layouts  58.7 us (12%)
  starting transfers between devices  43.8 us (9%)
  other arithmetic  31.6 us (6%)
  between operations  17.6 us (3%)
    psum x1, blocking collectives, body(): lax.psum((down_shard, up_shard), 'seq')  134 us
    psum x1, waiting for transfers between devices, body(): lax.psum(lax.psum((down_shard, up_shard), 'seq'), 'fsdp')  52.1 us
    psum x1, blocking collectives, body(): lax.psum(lax.psum((down_shard, up_shard), 'seq'), 'fsdp')  33.4 us
    dot_general x8, matrix products, body(): jnp.einsum('hqk,qhd->khd', probs_low, grad_block, preferred_element_type=...  22.6 us
    unnamed x280, local copies, waits for them, and re-layouts  22.3 us
    dot_general x8, matrix products, body(): jnp.einsum('hqk,qhd->khd', grad_scores, query_block, preferred_element_ty...  19.4 us
    all_to_all x1, waiting for transfers between devices, body(): lax.all_to_all(attention_output_gradient.reshape(shaped), 'seq', split_ax...  14.1 us
    slice x9, local copies, waits for them, and re-layouts, body(): query_block = head_query[first_row:finish]  13.6 us
  transfers between devices with their start and end apart: 10, of which 6 were waited for; matrix products, arithmetic and copies ran while one was open for 32% of the time, Pallas kernels for 0%

profile of v1, /device:TPU:2, one launch (start us, length us, event | category | flops | bytes accessed | tf_op | source)
XLA Modules:
  0.0 503.5 jit_solution(3713143607047965410)
XLA Ops:
  8.8 2.3 copy.161
  11.0 7.6 %all-to-all-start.2 = ((bf16[128,32,128]{0,2,1:T(8,128)(2,1)}), bf16[128,32,128]{0,2,1:T(8,128)(2,1)S(1)}, u32[]{:S(2)}, u32[]{:S(2)}) async-start(bf16[128,32,128]{0,2,1:T(8,128)(2,1)} %bitcast.418), calls=%async_computation.2 | async-start | bytes 2097152 | tf_op jit(solution)/shard_map/all_to_all | solution.py:65
  20.5 14.1 %all-to-all-done.2 = bf16[128,32,128]{0,2,1:T(8,128)(2,1)S(1)} async-done(((bf16[128,32,128]{0,2,1:T(8,128)(2,1)}), bf16[128,32,128]{0,2,1:T(8,128)(2,1)S(1)}, u32[]{:S(2)}, u32[]{:S(2)}) %all-to-all-start.2) | async-done | bytes 1048608 | tf_op jit(solution)/shard_map/all_to_all | solution.py:65
  36.0 5.2 %all-to-all-start.1 = ((bf16[128,32,128]{2,0,1:T(8,128)(2,1)}), bf16[128,32,128]{2,0,1:T(8,128)(2,1)S(1)}, u32[]{:S(2)}, u32[]{:S(2)}) async-start(bf16[128,32,128]{2,0,1:T(8,128)(2,1)} %bitcast.417), calls=%async_computation.1 | async-start | bytes 2097152 | tf_op jit(solution)/shard_map/all_to_all | solution.py:63
  41.8 2.3 copy.158
  49.1 8.2 %all-to-all-done.1 = bf16[128,32,128]{2,0,1:T(8,128)(2,1)S(1)} async-done(((bf16[128,32,128]{2,0,1:T(8,128)(2,1)}), bf16[128,32,128]{2,0,1:T(8,128)(2,1)S(1)}, u32[]{:S(2)}, u32[]{:S(2)}) %all-to-all-start.1) | async-done | bytes 1048608 | tf_op jit(solution)/shard_map/all_to_all | solution.py:63
  57.3 6.2 %all-to-all-start = ((bf16[128,32,128]{0,2,1:T(8,128)(2,1)}), bf16[128,32,128]{0,2,1:T(8,128)(2,1)}, u32[]{:S(2)}, u32[]{:S(2)}) async-start(bf16[128,32,128]{0,2,1:T(8,128)(2,1)} %bitcast.416), calls=%async_computation | async-start | bytes 2097152 | tf_op jit(solution)/shard_map/all_to_all | solution.py:60
  68.9 1.7 copy.162
  70.5 8.6 %all-to-all-done = bf16[128,32,128]{0,2,1:T(8,128)(2,1)} async-done(((bf16[128,32,128]{0,2,1:T(8,128)(2,1)}), bf16[128,32,128]{0,2,1:T(8,128)(2,1)}, u32[]{:S(2)}, u32[]{:S(2)}) %all-to-all-start) | async-done | bytes 1048608 | tf_op jit(solution)/shard_map/all_to_all | solution.py:60
  79.1 2.2 fusion.117
  81.4 1.7 copy.159
  83.0 1.7 copy.164
  84.7 1.7 copy.163
  86.4 1.7 copy.166
  88.0 1.7 copy.165
  89.7 1.7 copy.168
  91.3 1.7 copy.167
  98.4 1.7 copy.176
  100.1 1.7 copy.175
  101.8 1.4 fusion.121
  103.4 1.5 convolution_bitcast_fusion.14
  104.9 1.5 dynamic_update_slice.48
  116.0 1.5 fusion.17
  118.8 1.5 fusion.19
  120.3 1.6 fusion.69
  121.9 3.1 fusion.39
  125.0 3.1 fusion.41
  128.2 3.1 fusion.43
  131.3 3.1 fusion.45
  134.4 4.7 fusion.56
  140.7 5.1 %all-to-all-start.4 = ((bf16[128,32,128]{2,0,1:T(8,128)(2,1)}), bf16[128,32,128]{2,0,1:T(8,128)(2,1)S(1)}, u32[]{:S(2)}, u32[]{:S(2)}) async-start(bf16[128,32,128]{2,0,1:T(8,128)(2,1)} %bitcast.419), calls=%async_computation.4 | async-start | bytes 2097152 | tf_op jit(solution)/shard_map/all_to_all | solution.py:64
  145.8 4.1 fusion.47
  149.9 3.1 fusion.49
  153.0 8.8 %all-to-all-done.4 = bf16[128,32,128]{2,0,1:T(8,128)(2,1)S(1)} async-done(((bf16[128,32,128]{2,0,1:T(8,128)(2,1)}), bf16[128,32,128]{2,0,1:T(8,128)(2,1)S(1)}, u32[]{:S(2)}, u32[]{:S(2)}) %all-to-all-start.4) | async-done | bytes 1048608 | tf_op jit(solution)/shard_map/all_to_all | solution.py:64
  161.9 5.8 %all-to-all-start.3 = ((f32[4096,1,128]{2,1,0:T(1,128)}), f32[4096,1,128]{2,1,0:T(1,128)}, u32[]{:S(2)}, u32[]{:S(2)}) async-start(f32[4096,1,128]{2,1,0:T(1,128)} %bitcast.62), calls=%async_computation.3 | async-start | bytes 4194304 | tf_op jit(solution)/shard_map/all_to_all | solution.py:130
  172.8 2.5 multiply_reduce_fusion.5
  175.4 2.5 multiply_reduce_fusion.4
  183.6 1.4 multiply_reduce_fusion
  187.1 2.7 multiply_convert_fusion.5
  191.1 2.7 multiply_convert_fusion.4
  205.5 2.7 reduce.48
  209.3 1.5 fusion.72
  210.8 1.6 dynamic_update_slice.56
  213.6 2.6 fusion.37
  216.3 2.6 fusion.35
  218.9 7.8 %all-to-all-start.5 = ((bf16[32,2,8192]{2,1,0:T(2,128)(2,1)}), bf16[32,2,8192]{2,1,0:T(2,128)(2,1)S(1)}, u32[]{:S(2)}, u32[]{:S(2)}) async-start(bf16[32,2,8192]{2,1,0:T(2,128)(2,1)} %reshape.801), calls=%async_computation.5 | async-start | bytes 2097152 | tf_op jit(solution)/shard_map/all_to_all | solution.py:126
  226.8 3.3 fusion.33
  230.1 2.8 fusion.31
  232.9 2.7 fusion.29
  235.6 2.7 fusion.27
  238.2 4.4 all-to-all-done.5
  242.6 6.0 %all-to-all-start.6 = ((f32[4096,1,128]{2,1,0:T(1,128)}), f32[4096,1,128]{2,1,0:T(1,128)}, u32[]{:S(2)}, u32[]{:S(2)}) async-start(f32[4096,1,128]{2,1,0:T(1,128)} %bitcast.139), calls=%async_computation.6 | async-start | bytes 4194304 | tf_op jit(solution)/shard_map/all_to_all | solution.py:129
  248.6 2.4 reduce_sum.180
  253.9 134.4 %psum.30 = f32[16,512]{1,0:T(8,128)S(1)} all-reduce(f32[16,512]{1,0:T(8,128)S(1)} %convolution_multiply_fusion.25), channel_id=1, replica_groups=mesh['seq'=32,'fsdp'=8] {'seq'}, use_global_device_ids=true, to_apply=%region_30.31 | all-reduce | flops 8192 | bytes 65536 | tf_op jit(solution)/shard_map/psum | solution.py:172
  388.4 33.4 %psum.31 = f32[16,512]{1,0:T(8,128)} all-reduce(f32[16,512]{1,0:T(8,128)S(1)} %psum.30), channel_id=1, replica_groups=mesh['seq'=32,'fsdp'=8] {'fsdp'}, use_global_device_ids=true, to_apply=%region_31.32 | all-reduce | flops 8192 | bytes 65536 | tf_op jit(solution)/shard_map/psum | solution.py:171
  421.8 6.3 %fusion.105 = f32[128,8192]{1,0:T(8,128)S(1)} fusion(bf16[8192,512]{1,0:T(8,128)(2,1)} %all-gather.2.cloned.1.call-done, f32[128,512]{0,1:T(8,128)S(1)} %bitcast.414), kind=kOutput, calls=%fused_computation.176 | convolution fusion | flops 1073807360 | bytes 12845056 | tf_op jit(solution)/shard_map/dot_general | solution.py:14
  428.1 2.1 fusion.1
  430.1 3.4 reshape.802
  433.6 1.7 copy.200
  435.3 1.3 copy.188
  436.6 2.3 copy.191
  438.9 1.7 reduce_sum.189
  441.6 52.1 %all-reduce.7.cloned.1.call-done = f32[16,8192]{1,0:T(8,128)} async-done(((f32[16,8192]{1,0:T(8,128)}), f32[16,8192]{1,0:T(8,128)}) %all-reduce.7.cloned.1.call-update) | async-done | bytes 524304 | tf_op jit(solution)/shard_map/psum | solution.py:171
  493.7 1.9 copy.228
  (362 shorter events, 64.0 us)
Async XLA Ops:
  8.0 57.4 %copy-start = (bf16[1,128,8192]{2,1,0:T(8,128)(2,1)S(1)}, bf16[1,128,8192]{2,1,0:T(8,128)(2,1)}, u32[]{:S(2)}) copy-start(bf16[1,128,8192]{2,1,0:T(8,128)(2,1)} %param.8) | copy-start | bytes 6291460
  8.0 10.6 %copy-start.59 = (bf16[1,128,512]{2,1,0:T(8,128)(2,1)S(1)}, bf16[1,128,512]{2,1,0:T(8,128)(2,1)}, u32[]{:S(2)}) copy-start(bf16[1,128,512]{2,1,0:T(8,128)(2,1)} %param.10) | copy-start | bytes 393220
  8.0 126.4 %all-gather.2.cloned.1.call-start = ((), (), s32[]{:S(2)}) async-start(), calls=%async_computation.7 | async-start | bytes 9437184 | tf_op jit(solution)/shard_map/all_gather | solution.py:150
  11.0 23.6 %all-to-all-start.2 = ((bf16[128,32,128]{0,2,1:T(8,128)(2,1)}), bf16[128,32,128]{0,2,1:T(8,128)(2,1)S(1)}, u32[]{:S(2)}, u32[]{:S(2)}) async-start(bf16[128,32,128]{0,2,1:T(8,128)(2,1)} %bitcast.418), calls=%async_computation.2 | async-start | bytes 2097152 | tf_op jit(solution)/shard_map/all_to_all | solution.py:65
  18.7 25.4 %copy-start.135 = (s32[1,8]{1,0:T(1,128)S(1)}, s32[1,8]{1,0:T(1,128)}, u32[]{:S(2)}) copy-start(s32[1,8]{1,0:T(1,128)} %param.15) | copy-start | bytes 100
  36.0 29.4 %copy-start.34 = (bf16[16,8192]{1,0:T(8,128)(2,1)S(1)}, bf16[16,8192]{1,0:T(8,128)(2,1)}, u32[]{:S(2)}) copy-start(bf16[16,8192]{1,0:T(8,128)(2,1)} %param.13) | copy-start | bytes 786436
  36.0 21.3 %all-to-all-start.1 = ((bf16[128,32,128]{2,0,1:T(8,128)(2,1)}), bf16[128,32,128]{2,0,1:T(8,128)(2,1)S(1)}, u32[]{:S(2)}, u32[]{:S(2)}) async-start(bf16[128,32,128]{2,0,1:T(8,128)(2,1)} %bitcast.417), calls=%async_computation.1 | async-start | bytes 2097152 | tf_op jit(solution)/shard_map/all_to_all | solution.py:63
  49.1 19.8 %copy-start.44 = (s32[4096]{0:T(1024)}, s32[4096]{0:T(1024)S(1)}, u32[]{:S(2)}) copy-start(s32[4096]{0:T(1024)S(1)} %convert_reduce_fusion) | copy-start | bytes 49156
  57.3 21.9 %all-to-all-start = ((bf16[128,32,128]{0,2,1:T(8,128)(2,1)}), bf16[128,32,128]{0,2,1:T(8,128)(2,1)}, u32[]{:S(2)}, u32[]{:S(2)}) async-start(bf16[128,32,128]{0,2,1:T(8,128)(2,1)} %bitcast.416), calls=%async_computation | async-start | bytes 2097152 | tf_op jit(solution)/shard_map/all_to_all | solution.py:60
  63.5 4.5 copy-start.30
  68.9 32.9 %copy-start.126 = (s32[512]{0:T(512)S(1)}, s32[512]{0:T(512)}, u32[]{:S(2)}) copy-start(s32[512]{0:T(512)} %get-tuple-element.55) | copy-start | bytes 6148
  68.9 32.9 %copy-start.127 = (s32[512]{0:T(512)S(1)}, s32[512]{0:T(512)}, u32[]{:S(2)}) copy-start(s32[512]{0:T(512)} %get-tuple-element.94) | copy-start | bytes 6148
  103.1 3.2 copy-start.27
  103.1 3.2 copy-start.90
  103.3 3.0 copy-start.92
  103.3 3.0 copy-start.42
  103.3 3.0 slice-start
  107.1 13.2 %copy-start.14 = (f32[512,1024]{1,0:T(8,128)}, f32[512,1024]{1,0:T(8,128)S(1)}, u32[]{:S(2)}) copy-start(f32[512,1024]{1,0:T(8,128)S(1)} %get-tuple-element.65) | copy-start | bytes 6291460
  108.2 3.4 copy-start.51
  108.2 5.0 copy-start.49
  108.3 6.6 %copy-start.47 = (bf16[12,128,1,128]{3,1,0,2:T(8,128)(2,1)}, bf16[12,128,1,128]{3,1,0,2:T(8,128)(2,1)S(1)}, u32[]{:S(2)}) copy-start(bf16[12,128,1,128]{3,1,0,2:T(8,128)(2,1)S(1)} %get-tuple-element.27) | copy-start | bytes 1179652
  108.3 9.2 %copy-start.45 = (bf16[12,128,1,128]{3,1,0,2:T(8,128)(2,1)}, bf16[12,128,1,128]{3,1,0,2:T(8,128)(2,1)S(1)}, u32[]{:S(2)}) copy-start(bf16[12,128,1,128]{3,1,0,2:T(8,128)(2,1)S(1)} %get-tuple-element.26) | copy-start | bytes 1179652
  109.3 12.5 %copy-start.12 = (f32[512,1536]{1,0:T(8,128)}, f32[512,1536]{1,0:T(8,128)S(1)}, u32[]{:S(2)}) copy-start(f32[512,1536]{1,0:T(8,128)S(1)} %get-tuple-element.67) | copy-start | bytes 9437188
  109.3 12.5 %copy-start.105 = (f32[512]{0:T(512)}, f32[512]{0:T(512)S(1)}, u32[]{:S(2)}) copy-start(f32[512]{0:T(512)S(1)} %get-tuple-element.66) | copy-start | bytes 6148
  109.9 11.9 %copy-start.116 = (f32[512]{0:T(512)}, f32[512]{0:T(512)S(1)}, u32[]{:S(2)}) copy-start(f32[512]{0:T(512)S(1)} %fusion.9) | copy-start | bytes 6148
  111.0 14.0 %copy-start.10 = (f32[512,1536]{1,0:T(8,128)}, f32[512,1536]{1,0:T(8,128)S(1)}, u32[]{:S(2)}) copy-start(f32[512,1536]{1,0:T(8,128)S(1)} %get-tuple-element.69) | copy-start | bytes 9437188
  111.0 14.0 %copy-start.103 = (f32[512]{0:T(512)}, f32[512]{0:T(512)S(1)}, u32[]{:S(2)}) copy-start(f32[512]{0:T(512)S(1)} %get-tuple-element.68) | copy-start | bytes 6148
  111.6 13.4 %copy-start.114 = (f32[512]{0:T(512)}, f32[512]{0:T(512)S(1)}, u32[]{:S(2)}) copy-start(f32[512]{0:T(512)S(1)} %fusion.11) | copy-start | bytes 6148
  112.7 15.5 %copy-start.5 = (f32[512,1536]{1,0:T(8,128)}, f32[512,1536]{1,0:T(8,128)S(1)}, u32[]{:S(2)}) copy-start(f32[512,1536]{1,0:T(8,128)S(1)} %get-tuple-element.71) | copy-start | bytes 9437188
  112.7 15.5 %copy-start.98 = (f32[512]{0:T(512)}, f32[512]{0:T(512)S(1)}, u32[]{:S(2)}) copy-start(f32[512]{0:T(512)S(1)} %get-tuple-element.70) | copy-start | bytes 6148
  113.2 14.9 %copy-start.110 = (f32[512]{0:T(512)}, f32[512]{0:T(512)S(1)}, u32[]{:S(2)}) copy-start(f32[512]{0:T(512)S(1)} %fusion.13) | copy-start | bytes 6148
  114.3 17.0 %copy-start.3 = (f32[512,1536]{1,0:T(8,128)}, f32[512,1536]{1,0:T(8,128)S(1)}, u32[]{:S(2)}) copy-start(f32[512,1536]{1,0:T(8,128)S(1)} %get-tuple-element.73) | copy-start | bytes 9437188
  114.3 17.0 %copy-start.96 = (f32[512]{0:T(512)}, f32[512]{0:T(512)S(1)}, u32[]{:S(2)}) copy-start(f32[512]{0:T(512)S(1)} %get-tuple-element.72) | copy-start | bytes 6148
  114.9 16.4 %copy-start.108 = (f32[512]{0:T(512)}, f32[512]{0:T(512)S(1)}, u32[]{:S(2)}) copy-start(f32[512]{0:T(512)S(1)} %fusion.15) | copy-start | bytes 6148
  118.7 3.1 copy-start.7
  118.7 3.1 copy-start.100
  121.9 3.1 copy-start.69
  125.0 3.1 copy-start.67
  128.2 3.1 copy-start.65
  134.4 4.7 copy-start.75
  134.4 4.7 copy-start.76
  140.7 21.2 %all-to-all-start.4 = ((bf16[128,32,128]{2,0,1:T(8,128)(2,1)}), bf16[128,32,128]{2,0,1:T(8,128)(2,1)S(1)}, u32[]{:S(2)}, u32[]{:S(2)}) async-start(bf16[128,32,128]{2,0,1:T(8,128)(2,1)} %bitcast.419), calls=%async_computation.4 | async-start | bytes 2097152 | tf_op jit(solution)/shard_map/all_to_all | solution.py:64
  145.8 4.2 copy-start.8
  145.8 4.1 copy-start.61
  145.8 4.1 copy-start.101
  145.8 4.1 copy-start.112
  161.9 57.1 %all-to-all-start.3 = ((f32[4096,1,128]{2,1,0:T(1,128)}), f32[4096,1,128]{2,1,0:T(1,128)}, u32[]{:S(2)}, u32[]{:S(2)}) async-start(f32[4096,1,128]{2,1,0:T(1,128)} %bitcast.62), calls=%async_computation.3 | async-start | bytes 4194304 | tf_op jit(solution)/shard_map/all_to_all | solution.py:130
  189.8 4.0 copy-start.16
  209.2 3.1 copy-start.32
  209.2 3.1 copy-start.43
  209.2 4.4 copy-start.17
  209.3 4.4 copy-start.39
  212.4 3.9 copy-start.20
  212.4 3.9 copy-start.41
  218.9 23.7 %all-to-all-start.5 = ((bf16[32,2,8192]{2,1,0:T(2,128)(2,1)}), bf16[32,2,8192]{2,1,0:T(2,128)(2,1)S(1)}, u32[]{:S(2)}, u32[]{:S(2)}) async-start(bf16[32,2,8192]{2,1,0:T(2,128)(2,1)} %reshape.801), calls=%async_computation.5 | async-start | bytes 2097152 | tf_op jit(solution)/shard_map/all_to_all | solution.py:126
  226.8 3.3 copy-start.22
  226.8 6.1 %copy-start.24 = (bf16[512,1536]{1,0:T(8,128)(2,1)S(1)}, bf16[512,1536]{1,0:T(8,128)(2,1)}, u32[]{:S(2)}) copy-start(bf16[512,1536]{1,0:T(8,128)(2,1)} %copy-done.23) | copy-start | bytes 4718596
  230.1 5.5 %copy-start.26 = (bf16[512,1536]{1,0:T(8,128)(2,1)S(1)}, bf16[512,1536]{1,0:T(8,128)(2,1)}, u32[]{:S(2)}) copy-start(bf16[512,1536]{1,0:T(8,128)(2,1)} %copy-done.25) | copy-start | bytes 4718596
  230.1 5.5 %copy-start.37 = (bf16[4,128,1,128]{3,1,0,2:T(8,128)(2,1)S(1)}, bf16[4,128,1,128]{3,1,0,2:T(8,128)(2,1)}, u32[]{:S(2)}) copy-start(bf16[4,128,1,128]{3,1,0,2:T(8,128)(2,1)} %copy.175) | copy-start | bytes 393220
  242.6 9.5 %copy-start.77 = (bf16[16,512]{1,0:T(8,128)(2,1)S(1)}, bf16[16,512]{1,0:T(8,128)(2,1)}, u32[]{:S(2)}) copy-start(bf16[16,512]{1,0:T(8,128)(2,1)} %param.14) | copy-start | bytes 49156
  242.6 196.3 %all-to-all-start.6 = ((f32[4096,1,128]{2,1,0:T(1,128)}), f32[4096,1,128]{2,1,0:T(1,128)}, u32[]{:S(2)}, u32[]{:S(2)}) async-start(f32[4096,1,128]{2,1,0:T(1,128)} %bitcast.139), calls=%async_computation.6 | async-start | bytes 4194304 | tf_op jit(solution)/shard_map/all_to_all | solution.py:129
  248.6 173.2 %all-reduce.5.cloned.1.call-start = ((), (), s32[]{:S(2)}) async-start(), calls=%async_computation.8 | async-start | bytes 1048576 | tf_op jit(solution)/shard_map/psum | solution.py:172
  253.6 240.1 %all-reduce.7.cloned.1.call-start = ((), (), s32[]{:S(2)}) async-start(), calls=%async_computation.9 | async-start | bytes 1048576 | tf_op jit(solution)/shard_map/psum | solution.py:171
  421.8 6.3 %copy-start.35 = (bf16[16,8192]{1,0:T(8,128)(2,1)S(1)}, bf16[16,8192]{1,0:T(8,128)(2,1)}, u32[]{:S(2)}) copy-start(bf16[16,8192]{1,0:T(8,128)(2,1)} %param.13) | copy-start | bytes 786436
  (83 other events, 156.3 us)
Sparse Core Ops, SparseCore 0:
  10.6 97.0 all-gather.1
  421.9 71.7 all-reduce.6
Sparse Core Ops, SparseCore 1:
  253.7 121.8 all-reduce.4
